TPU v7x, 32 devices: a whole 2x2x4 slice. The times are simulated.
32 devices in a mesh: ctx: 4 (over z), dp: 2 (over x), expert: 4 (over y, core).
Axes of the slice: x: 2, y: 2, z: 4, core: 2. Of those that a mesh axis runs over, the one named last changes fastest.
Arguments:
- tokens: bfloat16 [8, 1024, 2048], P(('dp', 'expert'), 'ctx'), may hold values from -6 to 6
- routes: int32 [8, 1024, 8], P(('dp', 'expert'), 'ctx'), may hold values from 0 to 15, all different within a row; in each aligned block of 256 rows (0 to 255, 256 to 511, ..., all dimensions but the last counted through in order) at most 176 rows name the same one
- w_query: bfloat16 [2048, 2048], replicated, may hold values from -0.125 to 0.125
- w_key: bfloat16 [2048, 2048], replicated, may hold values from -0.125 to 0.125
- w_value: bfloat16 [2048, 2048], replicated, may hold values from -0.125 to 0.125
- w_out: bfloat16 [2048, 2048], replicated, may hold values from -3 to 3
- attn_gain: float32 [2048], replicated, may hold values from 0.5 to 1.5
- query_gain: float32 [2048], replicated, may hold values from 0.5 to 1.5
- key_gain: float32 [2048], replicated, may hold values from 0.5 to 1.5
- mlp_gain: float32 [2048], replicated, may hold values from 0.5 to 1.5
- router: bfloat16 [2048, 16], replicated, may hold values from -0.125 to 0.125
- w_gate: bfloat16 [16, 2048, 1024], P('expert'), may hold values from -0.125 to 0.125
- w_up: bfloat16 [16, 2048, 1024], P('expert'), may hold values from -0.125 to 0.125
- w_down: bfloat16 [16, 1024, 2048], P('expert'), may hold values from -1.5 to 1.5
- cotangent: bfloat16 [8, 1024, 2048], P(('dp', 'expert'), 'ctx'), may hold values from -6 to 6
Outputs:
- mixed: bfloat16 [8, 1024, 2048], P(('dp', 'expert'), 'ctx')
- input_grad: float32 [8, 1024, 2048], P(('dp', 'expert'), 'ctx')
- grad_query: float32 [2048, 2048], P(('ctx', 'dp', 'expert'))
- grad_key: float32 [2048, 2048], P(('ctx', 'dp', 'expert'))
- grad_value: float32 [2048, 2048], P(('ctx', 'dp', 'expert'))
- grad_out: float32 [2048, 2048], P(('ctx', 'dp', 'expert'))
- grad_attn_gain: float32 [2048], P(('ctx', 'dp', 'expert'))
- grad_query_gain: float32 [2048], P(('ctx', 'dp', 'expert'))
- grad_key_gain: float32 [2048], P(('ctx', 'dp', 'expert'))
- grad_mlp_gain: float32 [2048], P(('ctx', 'dp', 'expert'))
- grad_router: float32 [2048, 16], P(('ctx', 'dp', 'expert'))
- grad_gate: float32 [16, 2048, 1024], P('expert', ('ctx', 'dp'))
- grad_up: float32 [16, 2048, 1024], P('expert', ('ctx', 'dp'))
- grad_down: float32 [16, 1024, 2048], P('expert', ('ctx', 'dp'))
Inputs may be any that keep to these rules, and one draw needn't show every extreme that they name: `routes`: each row names 8 different experts. Within each device's aligned block of 256 tokens no expert is named by more than 176 tokens, and some block reaches that bound.
All inputs are finite; a program needn't handle non-finite values.
Results may differ from a plain program's by a relative error of at most 0.03.
Values may be sent and summed in bfloat16 or wider, within the bound.
No kernel may reach another device: no remote copies, remote signals or barrier semaphores. Data moves between devices by JAX's collectives and lax.ppermute only.
A program may use at most 448 MiB of HBM per device.

v0:
```python
import math

import jax
import jax.numpy as jnp
from jax import lax
from jax.sharding import PartitionSpec as P

HEADS = 16
HEAD_DIM = 128


EPSILON = 1e-05
FLOAT = jnp.float32
BRAIN = jnp.bfloat16


def norm_forward(values, gain):
    inverse = lax.rsqrt(jnp.mean(values * values, axis=-1, keepdims=True) + EPSILON)
    return (values * inverse * gain, inverse)


def norm_backward(values, inverse, gain, upstream):
    weighted = upstream * gain
    gain_grad = jnp.sum(upstream * values * inverse, axis=0)
    value_grad = inverse * weighted - values * inverse * inverse * inverse * jnp.mean(
        weighted * values, axis=-1, keepdims=True
    )
    return (value_grad, gain_grad)


def rope_tables(positions):
    halfway = HEAD_DIM // 2
    frequency = 10000.0 ** (-jnp.arange(halfway, dtype=FLOAT) * 2.0 / HEAD_DIM)
    angles = positions.astype(FLOAT)[:, None] * frequency[None, :]
    angles = jnp.concatenate([angles, angles], axis=1)
    return (jnp.cos(angles), jnp.sin(angles))


def rotated(heads_rows, cosine, sine_table):
    halfway = HEAD_DIM // 2
    turned = jnp.concatenate([-heads_rows[..., halfway:], heads_rows[..., :halfway]], axis=-1)
    return heads_rows * cosine[:, None, :] + turned * sine_table[:, None, :]


def rotated_back(grads, cosine, sine_table):
    halfway = HEAD_DIM // 2
    sined = grads * sine_table[:, None, :]
    return grads * cosine[:, None, :] + jnp.concatenate(
        [sined[..., halfway:], -sined[..., :halfway]], axis=-1
    )


def outer_sum(left, right):
    return lax.dot_general(left, right, (((0,), (0,)), ((), ())), preferred_element_type=FLOAT)


def times_transpose(left, right):
    return lax.dot_general(left, right, (((1,), (1,)), ((), ())), preferred_element_type=FLOAT)


def make_fold(query_heads, query_positions, score_scale):

    def fold_keys(carry, piece_pair, first_row):
        running_max, running_sum, running_out = carry
        key_rows, value_rows = piece_pair
        piece_rows = key_rows.shape[0]
        key_heads = key_rows.reshape(piece_rows, HEADS, HEAD_DIM)
        value_heads = value_rows.reshape(piece_rows, HEADS, HEAD_DIM)
        scores = (
            jnp.einsum("qhd,khd->hqk", query_heads, key_heads, preferred_element_type=FLOAT)
            * score_scale
        )
        key_positions = first_row + jnp.arange(piece_rows, dtype=jnp.int32)
        visible = (key_positions[None, :] <= query_positions[:, None])[None]
        scores = jnp.where(visible, scores, -1e30)
        new_max = jnp.maximum(running_max, jnp.max(scores, axis=-1))
        weights = jnp.where(visible, jnp.exp(scores - new_max[..., None]), 0.0)
        fading = jnp.exp(running_max - new_max)
        running_sum = running_sum * fading + jnp.sum(weights, axis=-1)
        running_out = running_out * fading[..., None] + jnp.einsum(
            "hqk,khd->hqd", weights.astype(BRAIN), value_heads, preferred_element_type=FLOAT
        )
        return (new_max, running_sum, running_out)

    return fold_keys


def shards(
    tokens,
    routes,
    w_query,
    w_key,
    w_value,
    w_out,
    attn_gain,
    query_gain,
    key_gain,
    mlp_gain,
    router,
    w_gate,
    w_up,
    w_down,
    cotangent,
):
    inputs = tokens[0].astype(FLOAT)
    rows, width = inputs.shape
    top_count = routes.shape[2]
    ctx_count = lax.axis_size("ctx")
    expert_devices = lax.axis_size("expert")
    local_experts = w_gate.shape[0]
    experts_all = local_experts * expert_devices
    capacity = (rows * top_count * 4 // (3 * experts_all) + 7) // 8 * 8
    length = rows * ctx_count
    key_block = math.gcd(length, 512)
    block_count = length // key_block
    score_scale = HEAD_DIM ** (-0.5)
    query_positions = lax.axis_index("ctx") * rows + jnp.arange(rows, dtype=jnp.int32)
    cosine, sine_table = rope_tables(query_positions)
    block_starts = jnp.arange(block_count, dtype=jnp.int32) * key_block
    attn_normed, attn_inverse = norm_forward(inputs, attn_gain)
    attn_in = attn_normed.astype(BRAIN)
    query_lin = jnp.dot(attn_in, w_query, preferred_element_type=FLOAT)
    key_lin = jnp.dot(attn_in, w_key, preferred_element_type=FLOAT)
    value_send = jnp.dot(attn_in, w_value, preferred_element_type=FLOAT).astype(BRAIN)
    query_normed, query_inverse = norm_forward(query_lin, query_gain)
    key_normed, key_inverse = norm_forward(key_lin, key_gain)
    query_heads = rotated(query_normed.reshape(rows, HEADS, HEAD_DIM), cosine, sine_table).astype(
        BRAIN
    )
    key_send = (
        rotated(key_normed.reshape(rows, HEADS, HEAD_DIM), cosine, sine_table)
        .astype(BRAIN)
        .reshape(rows, width)
    )
    fold_keys = make_fold(query_heads, query_positions, score_scale)
    start_state = (
        jnp.full((HEADS, rows), -1e30, FLOAT),
        jnp.zeros((HEADS, rows), FLOAT),
        jnp.zeros((HEADS, rows, HEAD_DIM), FLOAT),
    )
    all_keys, all_values = (
        lax.all_gather(key_send, "ctx", axis=0, tiled=True),
        lax.all_gather(value_send, "ctx", axis=0, tiled=True),
    )

    def scan_fold(carry, slab):
        return (fold_keys(carry, (slab[0], slab[1]), slab[2]), None)

    final_state, _ = lax.scan(
        scan_fold,
        start_state,
        (
            all_keys.reshape(block_count, key_block, width),
            all_values.reshape(block_count, key_block, width),
            block_starts,
        ),
    )
    final_max, final_sum, final_out = final_state
    attn_heads = final_out / final_sum[..., None]
    log_total = final_max + jnp.log(final_sum)
    attn_rows = attn_heads.transpose(1, 0, 2).reshape(rows, width).astype(BRAIN)
    hidden = inputs + jnp.dot(attn_rows, w_out, preferred_element_type=FLOAT)
    mlp_normed, mlp_inverse = norm_forward(hidden, mlp_gain)
    expert_in = mlp_normed.astype(BRAIN)
    logits = jnp.dot(expert_in, router, preferred_element_type=FLOAT)
    gate_probs = jax.nn.softmax(logits, axis=-1)
    picked = routes[0]
    onehot = picked[:, :, None] == jnp.arange(experts_all, dtype=jnp.int32)[None, None, :]
    onehot_float = onehot.astype(FLOAT)
    gate_values = jnp.sum(onehot_float * gate_probs[:, None, :], axis=-1)
    flat_table = onehot.reshape(rows * top_count, experts_all).astype(jnp.int32)
    earlier = jnp.cumsum(flat_table, axis=0) - flat_table
    slot_index = jnp.sum(earlier * flat_table, axis=1)
    gate_weights, up_weights, down_weights = (w_gate, w_up, w_down)
    buffer_shape = (expert_devices, local_experts, capacity, width)
    flat_index = picked.reshape(rows * top_count) * capacity + slot_index
    send_rows = (
        jnp.zeros((experts_all * capacity, width), BRAIN)
        .at[flat_index]
        .set(jnp.repeat(expert_in, top_count, axis=0))
        .reshape(buffer_shape)
    )
    received = lax.all_to_all(send_rows, "expert", split_axis=0, concat_axis=0, tiled=True)
    gate_pre = jnp.einsum("secd,edf->secf", received, gate_weights, preferred_element_type=FLOAT)
    up_pre = jnp.einsum("secd,edf->secf", received, up_weights, preferred_element_type=FLOAT)
    activated = (jax.nn.silu(gate_pre) * up_pre).astype(BRAIN)
    produced = jnp.einsum(
        "secf,efd->secd", activated, down_weights, preferred_element_type=FLOAT
    ).astype(BRAIN)
    produced, gate_pre, up_pre, received = (produced, gate_pre, up_pre, received)
    returned = lax.all_to_all(produced, "expert", split_axis=0, concat_axis=0, tiled=True)
    expert_rows = (
        returned.reshape(experts_all * capacity, width)[flat_index]
        .reshape(rows, top_count, width)
        .astype(FLOAT)
    )
    mixed = hidden + jnp.sum(gate_values[:, :, None] * expert_rows, axis=1)
    upstream = cotangent[0].astype(FLOAT)
    gate_grads = jnp.sum(upstream[:, None, :] * expert_rows, axis=-1)
    out_grads = (
        (gate_values[:, :, None] * upstream[:, None, :])
        .astype(BRAIN)
        .reshape(rows * top_count, width)
    )
    grad_send = (
        jnp.zeros((experts_all * capacity, width), BRAIN)
        .at[flat_index]
        .set(out_grads)
        .reshape(buffer_shape)
    )
    grad_received = lax.all_to_all(grad_send, "expert", split_axis=0, concat_axis=0, tiled=True)
    sigmoid_gate = jax.nn.sigmoid(gate_pre)
    silu_gate = jax.nn.silu(gate_pre)
    activated = (silu_gate * up_pre).astype(BRAIN)
    act_grad = jnp.einsum(
        "secd,efd->secf", grad_received, down_weights, preferred_element_type=FLOAT
    )
    up_grad = (act_grad * silu_gate).astype(BRAIN)
    gate_grad = (act_grad * up_pre * sigmoid_gate * (1.0 + gate_pre * (1.0 - sigmoid_gate))).astype(
        BRAIN
    )
    down_weight_grad = jnp.einsum(
        "secf,secd->efd", activated, grad_received, preferred_element_type=FLOAT
    )
    gate_weight_grad = jnp.einsum(
        "secd,secf->edf", received, gate_grad, preferred_element_type=FLOAT
    )
    up_weight_grad = jnp.einsum("secd,secf->edf", received, up_grad, preferred_element_type=FLOAT)
    input_rows = (
        jnp.einsum("secf,edf->secd", gate_grad, gate_weights, preferred_element_type=FLOAT)
        + jnp.einsum("secf,edf->secd", up_grad, up_weights, preferred_element_type=FLOAT)
    ).astype(BRAIN)
    returned_grads = lax.all_to_all(input_rows, "expert", split_axis=0, concat_axis=0, tiled=True)
    expert_in_grad = jnp.sum(
        returned_grads.reshape(experts_all * capacity, width)[flat_index]
        .reshape(rows, top_count, width)
        .astype(FLOAT),
        axis=1,
    )
    prob_grads = jnp.einsum("rk,rke->re", gate_grads, onehot_float)
    logit_grads = (
        gate_probs * (prob_grads - jnp.sum(prob_grads * gate_probs, axis=-1, keepdims=True))
    ).astype(BRAIN)
    router_grad = outer_sum(expert_in, logit_grads)
    expert_in_grad = expert_in_grad + times_transpose(logit_grads, router)
    hidden_part, mlp_gain_grad = norm_backward(hidden, mlp_inverse, mlp_gain, expert_in_grad)
    hidden_grad = upstream + hidden_part
    hidden_low = hidden_grad.astype(BRAIN)
    out_weight_grad = outer_sum(attn_rows, hidden_low)
    attn_grad = times_transpose(hidden_low, w_out).astype(BRAIN)
    attn_grad_heads = attn_grad.reshape(rows, HEADS, HEAD_DIM)
    row_delta = jnp.sum(attn_heads * attn_grad_heads.transpose(1, 0, 2).astype(FLOAT), axis=-1)

    def back_block(query_grad, slab):
        key_rows, value_rows, first_row = slab
        key_heads = key_rows.reshape(key_block, HEADS, HEAD_DIM)
        value_heads = value_rows.reshape(key_block, HEADS, HEAD_DIM)
        scores = (
            jnp.einsum("qhd,khd->hqk", query_heads, key_heads, preferred_element_type=FLOAT)
            * score_scale
        )
        key_positions = first_row + jnp.arange(key_block, dtype=jnp.int32)
        visible = (key_positions[None, :] <= query_positions[:, None])[None]
        probs_block = jnp.where(visible, jnp.exp(scores - log_total[..., None]), 0.0)
        prob_grad = jnp.einsum(
            "qhd,khd->hqk", attn_grad_heads, value_heads, preferred_element_type=FLOAT
        )
        score_grad = (probs_block * (prob_grad - row_delta[..., None])).astype(BRAIN)
        query_grad = query_grad + jnp.einsum(
            "hqk,khd->qhd", score_grad, key_heads, preferred_element_type=FLOAT
        )
        key_part = (
            jnp.einsum(
                "hqk,qhd->khd", score_grad, query_heads, preferred_element_type=FLOAT
            ).reshape(key_block, width)
            * score_scale
        )
        value_part = jnp.einsum(
            "hqk,qhd->khd", probs_block.astype(BRAIN), attn_grad_heads, preferred_element_type=FLOAT
        ).reshape(key_block, width)
        return (query_grad, (key_part, value_part))

    query_grad, (key_parts, value_parts) = lax.scan(
        back_block,
        jnp.zeros((rows, HEADS, HEAD_DIM), FLOAT),
        (
            all_keys.reshape(block_count, key_block, width),
            all_values.reshape(block_count, key_block, width),
            block_starts,
        ),
    )
    key_sums, value_sums = (
        lax.psum_scatter(
            key_parts.reshape(ctx_count, rows, width).astype(jnp.bfloat16),
            "ctx",
            scatter_dimension=0,
            tiled=True,
        ).astype(jnp.float32),
        lax.psum_scatter(
            value_parts.reshape(ctx_count, rows, width).astype(jnp.bfloat16),
            "ctx",
            scatter_dimension=0,
            tiled=True,
        ).astype(jnp.float32),
    )
    query_rot_grad = rotated_back(query_grad * score_scale, cosine, sine_table).reshape(rows, width)
    key_rot_grad = rotated_back(
        key_sums[0].reshape(rows, HEADS, HEAD_DIM), cosine, sine_table
    ).reshape(rows, width)
    query_lin_grad, query_gain_grad = norm_backward(
        query_lin, query_inverse, query_gain, query_rot_grad
    )
    key_lin_grad, key_gain_grad = norm_backward(key_lin, key_inverse, key_gain, key_rot_grad)
    query_low = query_lin_grad.astype(BRAIN)
    key_low = key_lin_grad.astype(BRAIN)
    value_low = value_sums[0].astype(BRAIN)
    query_weight_grad = outer_sum(attn_in, query_low)
    key_weight_grad = outer_sum(attn_in, key_low)
    value_weight_grad = outer_sum(attn_in, value_low)
    attn_in_grad = (
        times_transpose(query_low, w_query)
        + times_transpose(key_low, w_key)
        + times_transpose(value_low, w_value)
    )
    input_part, attn_gain_grad = norm_backward(inputs, attn_inverse, attn_gain, attn_in_grad)
    input_grad = hidden_grad + input_part
    gain_stack = jnp.stack([attn_gain_grad, query_gain_grad, key_gain_grad, mlp_gain_grad], axis=1)
    summed = (
        lax.psum_scatter(
            query_weight_grad, ("ctx", "dp", "expert"), scatter_dimension=0, tiled=True
        ),
        lax.psum_scatter(key_weight_grad, ("ctx", "dp", "expert"), scatter_dimension=0, tiled=True),
        lax.psum_scatter(
            value_weight_grad, ("ctx", "dp", "expert"), scatter_dimension=0, tiled=True
        ),
        lax.psum_scatter(out_weight_grad, ("ctx", "dp", "expert"), scatter_dimension=0, tiled=True),
        lax.psum_scatter(gain_stack, ("ctx", "dp", "expert"), scatter_dimension=0, tiled=True),
        lax.psum_scatter(router_grad, ("ctx", "dp", "expert"), scatter_dimension=0, tiled=True),
    )
    expert_summed = (
        lax.psum_scatter(
            gate_weight_grad.astype(jnp.bfloat16), ("ctx", "dp"), scatter_dimension=1, tiled=True
        ).astype(jnp.float32),
        lax.psum_scatter(
            up_weight_grad.astype(jnp.bfloat16), ("ctx", "dp"), scatter_dimension=1, tiled=True
        ).astype(jnp.float32),
        lax.psum_scatter(
            down_weight_grad.astype(jnp.bfloat16), ("ctx", "dp"), scatter_dimension=1, tiled=True
        ).astype(jnp.float32),
    )
    return (
        mixed.astype(BRAIN)[None],
        input_grad[None],
        summed[0],
        summed[1],
        summed[2],
        summed[3],
        summed[4][:, 0],
        summed[4][:, 1],
        summed[4][:, 2],
        summed[4][:, 3],
        summed[5],
        expert_summed[0],
        expert_summed[1],
        expert_summed[2],
    )


def solution(mesh):
    return jax.shard_map(
        shards,
        mesh=mesh,
        in_specs=(
            P(("dp", "expert"), "ctx", None),
            P(("dp", "expert"), "ctx", None),
            P(),
            P(),
            P(),
            P(),
            P(),
            P(),
            P(),
            P(),
            P(),
            P("expert", None, None),
            P("expert", None, None),
            P("expert", None, None),
            P(("dp", "expert"), "ctx", None),
        ),
        out_specs=(
            P(("dp", "expert"), "ctx", None),
            P(("dp", "expert"), "ctx", None),
            P(("ctx", "dp", "expert"), None),
            P(("ctx", "dp", "expert"), None),
            P(("ctx", "dp", "expert"), None),
            P(("ctx", "dp", "expert"), None),
            P(("ctx", "dp", "expert")),
            P(("ctx", "dp", "expert")),
            P(("ctx", "dp", "expert")),
            P(("ctx", "dp", "expert")),
            P(("ctx", "dp", "expert"), None),
            P("expert", ("ctx", "dp"), None),
            P("expert", ("ctx", "dp"), None),
            P("expert", ("ctx", "dp"), None),
        ),
        check_vma=False,
    )
```

profile of v0, /device:TPU:0, one launch (start us, length us, event | category | flops | bytes accessed | tf_op | source)
XLA Modules:
  0.0 2970.6 jit_solution(8409830536756451379)
XLA Ops:
  64.2 35.3 %all-gather.5.cloned.1.call-done = bf16[1024,2048]{1,0:T(8,128)(2,1)} async-done(((bf16[256,2048]{1,0:T(8,128)(2,1)}), bf16[1024,2048]{1,0:T(8,128)(2,1)}) %all-gather.5.cloned.1.call-update) | async-done | bytes 4194320 | tf_op jit(solution)/shard_map/all_gather | solution.py:143
  105.7 75.2 %all-gather.3.cloned.1.call-done = bf16[1024,2048]{1,0:T(8,128)(2,1)} async-done(((bf16[256,2048]{1,0:T(8,128)(2,1)}), bf16[1024,2048]{1,0:T(8,128)(2,1)}) %all-gather.3.cloned.1.call-update) | async-done | bytes 4194320 | tf_op jit(solution)/shard_map/all_gather | solution.py:142
  187.1 26.2 while.30
  273.7 104.4 %all-to-all-done = bf16[4,4,176,2048]{3,2,1,0:T(8,128)(2,1)} async-done(((bf16[4,4,176,2048]{3,2,1,0:T(8,128)(2,1)}), bf16[4,4,176,2048]{3,2,1,0:T(8,128)(2,1)}, u32[]{:S(2)}, u32[]{:S(2)}) %all-to-all-start) | async-done | bytes 11534368 | tf_op jit(solution)/shard_map/all_to_all | solution.py:183
  406.8 22.2 fusion.35
  429.0 82.4 %all-to-all-done.2 = bf16[4,4,176,2048]{3,2,1,0:T(8,128)(2,1)} async-done(((bf16[4,4,176,2048]{3,2,1,0:T(8,128)(2,1)}), bf16[4,4,176,2048]{3,2,1,0:T(8,128)(2,1)}, u32[]{:S(2)}, u32[]{:S(2)}) %all-to-all-start.2) | async-done | bytes 11534368 | tf_op jit(solution)/shard_map/all_to_all | solution.py:211
  511.4 29.7 %fusion.45 = (bf16[4,4,176,1024]{3,2,0,1:T(8,128)(2,1)}, bf16[4,4,176,1024]{3,2,0,1:T(8,128)(2,1)}, bf16[4,4,176,1024]{3,2,0,1:T(8,128)(2,1)}) fusion(f32[4,4,176,1024]{3,2,1,0:T(8,128)} %fusion.31, f32[4,4,176,1024]{3,2,1,0:T(8,128)} %fusion.35, bf16[4,1024,2048]{2,1,0:T(8,128)(2,1)} %param.32, bf16[4,4,176,2048]{3,2,1,0:T(8,128)(2,1)} %all-to-all-done.2), kind=kOutput, calls=%fused_computation.75 | convolution fusion | flops 11854413824 | bytes 68681728 | tf_op jit(solution)/shard_map/secd,efd->secf/dot_general | solution.py:215
  599.5 22.8 fusion.42
  632.2 73.6 %all-to-all-done.1 = bf16[4,4,176,2048]{3,2,1,0:T(8,128)(2,1)} async-done(((bf16[4,4,176,2048]{3,2,1,0:T(8,128)(2,1)}), bf16[4,4,176,2048]{3,2,1,0:T(8,128)(2,1)}, u32[]{:S(2)}, u32[]{:S(2)}) %all-to-all-start.1) | async-done | bytes 11534368 | tf_op jit(solution)/shard_map/all_to_all | solution.py:191
  712.0 22.2 gather_fusion
  744.0 94.7 %all-to-all-done.3 = bf16[4,4,176,2048]{3,2,1,0:T(8,128)(2,1)} async-done(((bf16[4,4,176,2048]{3,2,1,0:T(8,128)(2,1)}), bf16[4,4,176,2048]{3,2,1,0:T(8,128)(2,1)}, u32[]{:S(2)}, u32[]{:S(2)}) %all-to-all-start.3) | async-done | bytes 11534368 | tf_op jit(solution)/shard_map/all_to_all | solution.py:233
  838.7 22.3 gather_fusion.1
  884.9 51.5 %while.31 = (s32[]{:T(128)}, f32[256,16,128]{0,2,1:T(8,128)}, bf16[2,512,2048]{1,2,0:T(8,128)(2,1)}, bf16[2,512,2048]{2,1,0:T(8,128)(2,1)}, bf16[2,512,2048]{1,2...) while((s32[]{:T(128)}, f32[256,16,128]{0,2,1:T(8,128)}, ...), condition=%wide.region_23.24_spmd.clone, body=%wide.region_22.23_spmd.clone.sunk | while | flops 2708603648 | bytes 115792136 | solution.py:283
  967.2 49.9 %reduce-scatter.16.cloned.1.call-done = bf16[1,256,2048]{2,1,0:T(8,128)(2,1)} async-done(((bf16[4,256,2048]{2,1,0:T(8,128)(2,1)}), bf16[1,256,2048]{2,1,0:T(8,128)(2,1)}) %reduce-scatter.16.cloned.1.call-update) | async-done | bytes 1048592 | tf_op jit(solution)/shard_map/reduce_scatter | solution.py:293
  1035.4 61.2 %reduce-scatter.18.cloned.1.call-done = bf16[1,256,2048]{2,1,0:T(8,128)(2,1)} async-done(((bf16[4,256,2048]{2,1,0:T(8,128)(2,1)}), bf16[1,256,2048]{2,1,0:T(8,128)(2,1)}) %reduce-scatter.18.cloned.1.call-update) | async-done | bytes 1048592 | tf_op jit(solution)/shard_map/reduce_scatter | solution.py:299
  1206.2 29.6 reduce-scatter.36.cloned.1.call-done
  1240.8 130.2 %reduce-scatter.34.cloned.1.call-done = f32[64,4]{1,0:T(8,128)} async-done(((f32[2048,4]{1,0:T(8,128)}), f32[64,4]{1,0:T(8,128)}) %reduce-scatter.34.cloned.1.call-update) | async-done | bytes 1040
  1374.4 276.1 %reduce-scatter.32.cloned.1.call-done = bf16[4,128,2048]{2,1,0:T(8,128)(2,1)} async-done(((bf16[4,1024,2048]{2,1,0:T(8,128)(2,1)}), bf16[4,128,2048]{2,1,0:T(8,128)(2,1)}) %reduce-scatter.32.cloned.1.call-update) | async-done | bytes 2097168 | tf_op jit(solution)/shard_map/reduce_scatter | solution.py:347
  1654.5 278.6 %reduce-scatter.28.cloned.1.call-done = bf16[4,256,1024]{2,1,0:T(8,128)(2,1)} async-done(((bf16[4,2048,1024]{2,1,0:T(8,128)(2,1)}), bf16[4,256,1024]{2,1,0:T(8,128)(2,1)}) %reduce-scatter.28.cloned.1.call-update) | async-done | bytes 2097168 | tf_op jit(solution)/shard_map/reduce_scatter | solution.py:341
  1937.2 278.6 %reduce-scatter.30.cloned.1.call-done = bf16[4,256,1024]{2,1,0:T(8,128)(2,1)} async-done(((bf16[4,2048,1024]{2,1,0:T(8,128)(2,1)}), bf16[4,256,1024]{2,1,0:T(8,128)(2,1)}) %reduce-scatter.30.cloned.1.call-update) | async-done | bytes 2097168 | tf_op jit(solution)/shard_map/reduce_scatter | solution.py:344
  2219.9 181.0 %reduce-scatter.26.cloned.1.call-done = f32[64,2048]{1,0:T(8,128)} async-done(((f32[2048,2048]{1,0:T(8,128)}), f32[64,2048]{1,0:T(8,128)}) %reduce-scatter.26.cloned.1.call-update) | async-done | bytes 524304 | tf_op jit(solution)/shard_map/reduce_scatter | solution.py:336
  2400.8 187.5 %reduce-scatter.20.cloned.1.call-done = f32[64,2048]{1,0:T(8,128)} async-done(((f32[2048,2048]{1,0:T(8,128)}), f32[64,2048]{1,0:T(8,128)}) %reduce-scatter.20.cloned.1.call-update) | async-done | bytes 524304 | tf_op jit(solution)/shard_map/reduce_scatter | solution.py:329
  2588.3 187.4 %reduce-scatter.24.cloned.1.call-done = f32[64,2048]{1,0:T(8,128)} async-done(((f32[2048,2048]{1,0:T(8,128)}), f32[64,2048]{1,0:T(8,128)}) %reduce-scatter.24.cloned.1.call-update) | async-done | bytes 524304 | tf_op jit(solution)/shard_map/reduce_scatter | solution.py:333
  2775.7 188.2 %reduce-scatter.22.cloned.1.call-done = f32[64,2048]{1,0:T(8,128)} async-done(((f32[2048,2048]{1,0:T(8,128)}), f32[64,2048]{1,0:T(8,128)}) %reduce-scatter.22.cloned.1.call-update) | async-done | bytes 524304 | tf_op jit(solution)/shard_map/reduce_scatter | solution.py:332
  (352 shorter events, 521.7 us)
Async XLA Ops:
  7.2 245.6 %copy-start = (bf16[2048,16]{0,1:T(8,128)(2,1)S(1)}, bf16[2048,16]{0,1:T(8,128)(2,1)}, u32[]{:S(2)}) copy-start(bf16[2048,16]{0,1:T(8,128)(2,1)} %param.29) | copy-start | bytes 196612
  7.2 92.3 %all-gather.5.cloned.1.call-start = ((), (), s32[]{:S(2)}) async-start(), calls=%async_computation.16 | async-start | bytes 5242880 | tf_op jit(solution)/shard_map/all_gather | solution.py:143
  15.9 165.0 %all-gather.3.cloned.1.call-start = ((), (), s32[]{:S(2)}) async-start(), calls=%async_computation.15 | async-start | bytes 5242880 | tf_op jit(solution)/shard_map/all_gather | solution.py:142
  64.2 190.2 %copy-start.56 = (s32[2048,1]{0,1:T(1,128)}, s32[2048,1]{0,1:T(1,128)S(1)}, u32[]{:S(2)}) copy-start(s32[2048,1]{0,1:T(1,128)S(1)} %compare_select_fusion) | copy-start | bytes 24580
  245.0 133.1 %all-to-all-start = ((bf16[4,4,176,2048]{3,2,1,0:T(8,128)(2,1)}), bf16[4,4,176,2048]{3,2,1,0:T(8,128)(2,1)}, u32[]{:S(2)}, u32[]{:S(2)}) async-start(bf16[4,4,176,2048]{3,2,1,0:T(8,128)(2,1)} %bitcast.355), calls=%async_computation | async-start | bytes 23068672 | tf_op jit(solution)/shard_map/all_to_all | solution.py:183
  378.2 133.3 %all-to-all-start.2 = ((bf16[4,4,176,2048]{3,2,1,0:T(8,128)(2,1)}), bf16[4,4,176,2048]{3,2,1,0:T(8,128)(2,1)}, u32[]{:S(2)}, u32[]{:S(2)}) async-start(bf16[4,4,176,2048]{3,2,1,0:T(8,128)(2,1)} %bitcast.356), calls=%async_computation.2 | async-start | bytes 23068672 | tf_op jit(solution)/shard_map/all_to_all | solution.py:211
  572.5 133.2 %all-to-all-start.1 = ((bf16[4,4,176,2048]{3,2,1,0:T(8,128)(2,1)}), bf16[4,4,176,2048]{3,2,1,0:T(8,128)(2,1)}, u32[]{:S(2)}, u32[]{:S(2)}) async-start(bf16[4,4,176,2048]{3,2,1,0:T(8,128)(2,1)} %copy.161), calls=%async_computation.1 | async-start | bytes 23068672 | tf_op jit(solution)/shard_map/all_to_all | solution.py:191
  632.2 79.8 %copy-start.57 = (s32[2048,1]{0,1:T(1,128)S(1)}, s32[2048,1]{0,1:T(1,128)}, u32[]{:S(2)}) copy-start(s32[2048,1]{0,1:T(1,128)} %copy-done.56) | copy-start | bytes 24580
  632.2 79.8 %copy-start.32 = (f32[16,256]{1,0:T(8,128)S(1)}, f32[16,256]{1,0:T(8,128)}, u32[]{:S(2)}) copy-start(f32[16,256]{1,0:T(8,128)} %copy-done.31) | copy-start | bytes 49156
  632.2 79.8 %copy-start.38 = (f32[16,256]{1,0:T(8,128)S(1)}, f32[16,256]{1,0:T(8,128)}, u32[]{:S(2)}) copy-start(f32[16,256]{1,0:T(8,128)} %copy-done.37) | copy-start | bytes 49156
  705.7 133.0 %all-to-all-start.3 = ((bf16[4,4,176,2048]{3,2,1,0:T(8,128)(2,1)}), bf16[4,4,176,2048]{3,2,1,0:T(8,128)(2,1)}, u32[]{:S(2)}, u32[]{:S(2)}) async-start(bf16[4,4,176,2048]{3,2,1,0:T(8,128)(2,1)} %copy.164), calls=%async_computation.3 | async-start | bytes 23068672 | tf_op jit(solution)/shard_map/all_to_all | solution.py:233
  711.9 305.3 %reduce-scatter.16.cloned.1.call-start = ((), (), s32[]{:S(2)}) async-start(), calls=%async_computation.17 | async-start | bytes 5242880 | tf_op jit(solution)/shard_map/reduce_scatter | solution.py:293
  942.6 154.0 %reduce-scatter.18.cloned.1.call-start = ((), (), s32[]{:S(2)}) async-start(), calls=%async_computation.18 | async-start | bytes 5242880 | tf_op jit(solution)/shard_map/reduce_scatter | solution.py:299
  943.2 292.6 %reduce-scatter.36.cloned.1.call-start = ((), (), s32[]{:S(2)}) async-start(), calls=%async_computation.27 | async-start | bytes 1081344
  967.2 403.9 %reduce-scatter.34.cloned.1.call-start = ((), (), s32[]{:S(2)}) async-start(), calls=%async_computation.26 | async-start | bytes 1081344
  1035.4 69.6 %copy-start.55 = (f32[2048]{0:T(1024)S(1)}, f32[2048]{0:T(1024)}, u32[]{:S(2)}) copy-start(f32[2048]{0:T(1024)} %get-tuple-element.298) | copy-start | bytes 24580
  1106.4 544.0 %reduce-scatter.32.cloned.1.call-start = ((), (), s32[]{:S(2)}) async-start(), calls=%async_computation.25 | async-start | bytes 18874368 | tf_op jit(solution)/shard_map/reduce_scatter | solution.py:347
  1127.0 806.2 %reduce-scatter.28.cloned.1.call-start = ((), (), s32[]{:S(2)}) async-start(), calls=%async_computation.23 | async-start | bytes 18874368 | tf_op jit(solution)/shard_map/reduce_scatter | solution.py:341
  1146.5 1069.3 %reduce-scatter.30.cloned.1.call-start = ((), (), s32[]{:S(2)}) async-start(), calls=%async_computation.24 | async-start | bytes 18874368 | tf_op jit(solution)/shard_map/reduce_scatter | solution.py:344
  1166.4 1234.4 %reduce-scatter.26.cloned.1.call-start = ((), (), s32[]{:S(2)}) async-start(), calls=%async_computation.22 | async-start | bytes 17301504 | tf_op jit(solution)/shard_map/reduce_scatter | solution.py:336
  1177.3 1411.0 %reduce-scatter.20.cloned.1.call-start = ((), (), s32[]{:S(2)}) async-start(), calls=%async_computation.19 | async-start | bytes 17301504 | tf_op jit(solution)/shard_map/reduce_scatter | solution.py:329
  1186.9 1588.8 %reduce-scatter.24.cloned.1.call-start = ((), (), s32[]{:S(2)}) async-start(), calls=%async_computation.21 | async-start | bytes 17301504 | tf_op jit(solution)/shard_map/reduce_scatter | solution.py:333
  1196.5 1767.4 %reduce-scatter.22.cloned.1.call-start = ((), (), s32[]{:S(2)}) async-start(), calls=%async_computation.20 | async-start | bytes 17301504 | tf_op jit(solution)/shard_map/reduce_scatter | solution.py:332
  1933.1 1030.8 %copy-start.1 = (bf16[2048,16]{0,1:T(8,128)(2,1)S(1)}, bf16[2048,16]{0,1:T(8,128)(2,1)}, u32[]{:S(2)}) copy-start(bf16[2048,16]{0,1:T(8,128)(2,1)} %param.29) | copy-start | bytes 196612
  (71 other events, 730.3 us)
Sparse Core Ops, SparseCore 0:
  16.0 83.4 all-gather.4
  101.6 79.2 all-gather.2
  942.8 74.3 reduce-scatter.15
  1019.3 77.2 reduce-scatter.17
  1098.7 137.0 reduce-scatter.35
  1238.4 132.5 reduce-scatter.33
  1374.8 275.5 reduce-scatter.31
  1654.2 278.8 reduce-scatter.27
  1936.9 278.8 reduce-scatter.29
  2218.5 182.2 reduce-scatter.25
  2403.7 184.5 reduce-scatter.19
  2591.1 184.5 reduce-scatter.23
  2778.6 185.3 reduce-scatter.21
where the time goes:
time: 2980 us; the launch traced here: 2970 us
  waiting for transfers between devices  2310 us (78%)
  matrix products  327 us (11%)
  local copies, waits for them, and re-layouts  181 us (6%)
  other arithmetic  106 us (4%)
    reduce_scatter x1, waiting for transfers between devices, shards(): lax.psum_scatter(gate_weight_grad.astype(jnp.bfloat16), ('ctx', 'dp'), sc...  279 us
    reduce_scatter x1, waiting for transfers between devices, shards(): lax.psum_scatter(up_weight_grad.astype(jnp.bfloat16), ('ctx', 'dp'), scat...  279 us
    reduce_scatter x1, waiting for transfers between devices, shards(): lax.psum_scatter(down_weight_grad.astype(jnp.bfloat16), ('ctx', 'dp'), sc...  276 us
    reduce_scatter x1, waiting for transfers between devices, shards(): lax.psum_scatter(key_weight_grad, ('ctx', 'dp', 'expert'), scatter_dimens...  188 us
    reduce_scatter x1, waiting for transfers between devices, shards(): lax.psum_scatter(query_weight_grad, ('ctx', 'dp', 'expert'), scatter_dime...  188 us
    reduce_scatter x1, waiting for transfers between devices, shards(): lax.psum_scatter(value_weight_grad, ('ctx', 'dp', 'expert'), scatter_dime...  187 us
    reduce_scatter x1, waiting for transfers between devices, shards(): lax.psum_scatter(out_weight_grad, ('ctx', 'dp', 'expert'), scatter_dimens...  181 us
    unnamed x15, waiting for transfers between devices  160 us
  transfers between devices with their start and end apart: 17, of which 17 were waited for; matrix products, arithmetic and copies ran while one was open for 12% of the time, Pallas kernels for 0%

commit v1 on v0

v1 whole, which is shorter than its diff:
```python
import jax
import jax.numpy as jnp
from jax import lax
from jax.sharding import PartitionSpec as P

HEADS = 16
HEAD_DIM = 128


EPSILON = 1e-05
FLOAT = jnp.float32
BRAIN = jnp.bfloat16


def norm_inverse(values):
    return lax.rsqrt(jnp.mean(values * values, axis=-1, keepdims=True) + EPSILON)


def norm_backward(values, inverse, gain, upstream):
    weighted = upstream * gain
    gain_grad = jnp.sum(upstream * values * inverse, axis=0)
    value_grad = inverse * weighted - values * inverse * inverse * inverse * jnp.mean(
        weighted * values, axis=-1, keepdims=True
    )
    return (value_grad, gain_grad)


def rope_tables(positions):
    halfway = HEAD_DIM // 2
    frequency = 10000.0 ** (-jnp.arange(halfway, dtype=FLOAT) * 2.0 / HEAD_DIM)
    angles = positions.astype(FLOAT)[:, None] * frequency[None, :]
    angles = jnp.concatenate([angles, angles], axis=1)
    return (jnp.cos(angles), jnp.sin(angles))


def rotated(heads_rows, cosine, sine_table):
    halfway = HEAD_DIM // 2
    turned = jnp.concatenate([-heads_rows[..., halfway:], heads_rows[..., :halfway]], axis=-1)
    return heads_rows * cosine[:, None, :] + turned * sine_table[:, None, :]


def rotated_back(grads, cosine, sine_table):
    halfway = HEAD_DIM // 2
    sined = grads * sine_table[:, None, :]
    return grads * cosine[:, None, :] + jnp.concatenate(
        [sined[..., halfway:], -sined[..., :halfway]], axis=-1
    )


def outer_sum(left, right):
    return lax.dot_general(left, right, (((0,), (0,)), ((), ())), preferred_element_type=FLOAT)


def times_transpose(left, right):
    return lax.dot_general(left, right, (((1,), (1,)), ((), ())), preferred_element_type=FLOAT)


def times(left, right):
    return jnp.dot(left, right, preferred_element_type=FLOAT)


def shards(
    tokens,
    routes,
    w_query,
    w_key,
    w_value,
    w_out,
    attn_gain,
    query_gain,
    key_gain,
    mlp_gain,
    router,
    w_gate,
    w_up,
    w_down,
    cotangent,
):
    inputs = tokens[0].astype(FLOAT)
    rows, width = inputs.shape
    ctx_count = lax.axis_size("ctx")
    dp_count = lax.axis_size("dp")
    expert_devices = lax.axis_size("expert")
    plane = ("dp", "expert")
    plane_count = dp_count * expert_devices
    everything = ("ctx", "dp", "expert")
    local_experts = w_gate.shape[0]
    experts_all = local_experts * expert_devices
    own_experts = local_experts // dp_count
    length = rows * ctx_count
    heads = HEADS // ctx_count
    columns = heads * HEAD_DIM
    score_scale = HEAD_DIM ** (-0.5)
    ctx_at = lax.axis_index("ctx")
    dp_at = lax.axis_index("dp")
    expert_at = lax.axis_index("expert")
    first_column = ctx_at * columns

    attn_inverse = norm_inverse(inputs)
    attn_in = (inputs * attn_inverse * attn_gain).astype(BRAIN)
    all_in = lax.all_gather(attn_in, "ctx", axis=0, tiled=True)
    upstream_low = cotangent[0]
    upstream = upstream_low.astype(FLOAT)
    all_upstream = lax.all_gather(upstream_low, plane, axis=0, tiled=True)

    qkv_weights = jnp.concatenate(
        [
            lax.dynamic_slice_in_dim(weights, first_column, columns, axis=1)
            for weights in (w_query, w_key, w_value)
        ],
        axis=1,
    )
    out_weights = lax.dynamic_slice_in_dim(w_out, first_column, columns, axis=0)
    query_gain_own = lax.dynamic_slice_in_dim(query_gain, first_column, columns, axis=0)
    key_gain_own = lax.dynamic_slice_in_dim(key_gain, first_column, columns, axis=0)
    inverses = jnp.concatenate(
        [norm_inverse(times(attn_in, w_query)), norm_inverse(times(attn_in, w_key))], axis=1
    )
    all_inverses = lax.all_gather(inverses, "ctx", axis=0, tiled=True)
    query_inverse = all_inverses[:, 0:1]
    key_inverse = all_inverses[:, 1:2]
    cosine, sine_table = rope_tables(jnp.arange(length, dtype=jnp.int32))

    gate_weights, up_weights, down_weights = [
        lax.dynamic_slice_in_dim(weights, dp_at * own_experts, own_experts, axis=0)
        for weights in (w_gate, w_up, w_down)
    ]
    down_back = jnp.einsum(
        "td,efd->etf", all_upstream, down_weights, preferred_element_type=FLOAT
    )

    qkv_lin = times(all_in, qkv_weights)
    query_lin = qkv_lin[:, :columns]
    key_lin = qkv_lin[:, columns : 2 * columns]
    value_heads = qkv_lin[:, 2 * columns :].astype(BRAIN).reshape(length, heads, HEAD_DIM)
    query_heads = rotated(
        (query_lin * query_inverse * query_gain_own).reshape(length, heads, HEAD_DIM),
        cosine,
        sine_table,
    ).astype(BRAIN)
    key_heads = rotated(
        (key_lin * key_inverse * key_gain_own).reshape(length, heads, HEAD_DIM), cosine, sine_table
    ).astype(BRAIN)
    positions = jnp.arange(length, dtype=jnp.int32)
    visible = (positions[None, :] <= positions[:, None])[None]
    scores = (
        jnp.einsum("qhd,khd->hqk", query_heads, key_heads, preferred_element_type=FLOAT)
        * score_scale
    )
    scores = jnp.where(visible, scores, -1e30)
    probs = jax.nn.softmax(scores, axis=-1)
    probs_low = probs.astype(BRAIN)
    attn_wide = jnp.einsum("hqk,khd->qhd", probs_low, value_heads, preferred_element_type=FLOAT)
    attn_own = attn_wide.astype(BRAIN).reshape(length, columns)
    attn_rows = lax.all_to_all(attn_own, "ctx", split_axis=0, concat_axis=1, tiled=True)
    hidden = inputs + times(attn_rows, w_out)
    mlp_inverse = norm_inverse(hidden)
    expert_in = (hidden * mlp_inverse * mlp_gain).astype(BRAIN)
    all_expert_in = lax.all_gather(expert_in, plane, axis=0, tiled=True)
    logits = times(expert_in, router)
    gate_probs = jax.nn.softmax(logits, axis=-1)
    chosen = jnp.any(
        routes[0][:, :, None] == jnp.arange(experts_all, dtype=jnp.int32)[None, None, :], axis=1
    )
    gates = jnp.where(chosen, gate_probs, 0.0)
    all_gates = lax.all_gather(gates, plane, axis=0, tiled=True)
    first_expert = expert_at * local_experts + dp_at * own_experts
    own_gates = lax.dynamic_slice_in_dim(all_gates, first_expert, own_experts, axis=1).T[:, :, None]

    gate_pre = jnp.einsum(
        "td,edf->etf", all_expert_in, gate_weights, preferred_element_type=FLOAT
    )
    up_pre = jnp.einsum("td,edf->etf", all_expert_in, up_weights, preferred_element_type=FLOAT)
    sigmoid_gate = jax.nn.sigmoid(gate_pre)
    silu_gate = gate_pre * sigmoid_gate
    activated = silu_gate * up_pre
    weighted = (own_gates * activated).astype(BRAIN)
    own_gate_grads = jnp.sum(down_back * activated, axis=-1).T
    act_grad = own_gates * down_back
    up_grad = (act_grad * silu_gate).astype(BRAIN)
    gate_grad = (act_grad * up_pre * sigmoid_gate * (1.0 + gate_pre * (1.0 - sigmoid_gate))).astype(
        BRAIN
    )
    input_rows = (
        jnp.einsum("etf,edf->td", gate_grad, gate_weights, preferred_element_type=FLOAT)
        + jnp.einsum("etf,edf->td", up_grad, up_weights, preferred_element_type=FLOAT)
    ).astype(BRAIN)
    expert_in_grad = lax.psum_scatter(input_rows, plane, scatter_dimension=0, tiled=True).astype(
        FLOAT
    )
    produced = jnp.einsum(
        "etf,efd->td", weighted, down_weights, preferred_element_type=FLOAT
    ).astype(BRAIN)
    mixed = hidden + lax.psum_scatter(produced, plane, scatter_dimension=0, tiled=True).astype(
        FLOAT
    )
    gate_grads = lax.all_to_all(
        own_gate_grads.reshape(plane_count, rows, own_experts),
        plane,
        split_axis=0,
        concat_axis=0,
        tiled=True,
    )
    gate_grads = (
        gate_grads.reshape(dp_count, expert_devices, rows, own_experts)
        .transpose(2, 1, 0, 3)
        .reshape(rows, experts_all)
    )

    def spread(partial):
        summed = lax.psum_scatter(partial.astype(BRAIN), "ctx", scatter_dimension=1, tiled=True)
        return lax.all_to_all(summed, "dp", split_axis=1, concat_axis=0, tiled=True).astype(FLOAT)

    down_weight_grad = spread(
        jnp.einsum("etf,td->efd", weighted, all_upstream, preferred_element_type=FLOAT)
    )
    gate_weight_grad = spread(
        jnp.einsum("td,etf->edf", all_expert_in, gate_grad, preferred_element_type=FLOAT)
    )
    up_weight_grad = spread(
        jnp.einsum("td,etf->edf", all_expert_in, up_grad, preferred_element_type=FLOAT)
    )

    prob_grads = jnp.where(chosen, gate_grads, 0.0)
    logit_grads = (
        gate_probs * (prob_grads - jnp.sum(prob_grads * gate_probs, axis=-1, keepdims=True))
    ).astype(BRAIN)
    router_grad = outer_sum(expert_in, logit_grads)
    expert_in_grad = expert_in_grad + times_transpose(logit_grads, router)
    hidden_part, mlp_gain_grad = norm_backward(hidden, mlp_inverse, mlp_gain, expert_in_grad)
    hidden_grad = upstream + hidden_part
    hidden_low = hidden_grad.astype(BRAIN)
    all_hidden_low = lax.all_gather(hidden_low, "ctx", axis=0, tiled=True)
    attn_grad = times_transpose(all_hidden_low, out_weights).astype(BRAIN)
    attn_grad_heads = attn_grad.reshape(length, heads, HEAD_DIM)
    out_weight_grad = lax.psum_scatter(
        outer_sum(attn_own, all_hidden_low).astype(BRAIN), plane, scatter_dimension=0, tiled=True
    ).astype(FLOAT)
    row_delta = jnp.sum(attn_wide * attn_grad_heads.astype(FLOAT), axis=-1).T
    prob_grad = jnp.einsum(
        "qhd,khd->hqk", attn_grad_heads, value_heads, preferred_element_type=FLOAT
    )
    score_grad = (probs * (prob_grad - row_delta[..., None])).astype(BRAIN)
    query_grad = (
        jnp.einsum("hqk,khd->qhd", score_grad, key_heads, preferred_element_type=FLOAT)
        * score_scale
    )
    key_grad = (
        jnp.einsum("hqk,qhd->khd", score_grad, query_heads, preferred_element_type=FLOAT)
        * score_scale
    )
    value_low = (
        jnp.einsum("hqk,qhd->khd", probs_low, attn_grad_heads, preferred_element_type=FLOAT)
        .astype(BRAIN)
        .reshape(length, columns)
    )
    query_rot_grad = rotated_back(query_grad, cosine, sine_table).reshape(length, columns)
    key_rot_grad = rotated_back(key_grad, cosine, sine_table).reshape(length, columns)
    query_weighted = query_rot_grad * query_gain_own
    key_weighted = key_rot_grad * key_gain_own
    dots = lax.psum(
        jnp.stack(
            [jnp.sum(query_weighted * query_lin, axis=-1), jnp.sum(key_weighted * key_lin, axis=-1)]
        ),
        "ctx",
    ) * (1.0 / width)
    query_gain_grad = jnp.sum(query_rot_grad * query_lin * query_inverse, axis=0)
    key_gain_grad = jnp.sum(key_rot_grad * key_lin * key_inverse, axis=0)
    query_low = (
        query_inverse * query_weighted
        - query_lin * (query_inverse * query_inverse * query_inverse * dots[0][:, None])
    ).astype(BRAIN)
    key_low = (
        key_inverse * key_weighted
        - key_lin * (key_inverse * key_inverse * key_inverse * dots[1][:, None])
    ).astype(BRAIN)
    qkv_low = jnp.concatenate([query_low, key_low, value_low], axis=1)
    attn_in_grad = lax.psum_scatter(
        times_transpose(qkv_low, qkv_weights).astype(BRAIN), "ctx", scatter_dimension=0, tiled=True
    ).astype(FLOAT)
    qkv_weight_grad = outer_sum(all_in, qkv_low).astype(BRAIN)
    qkv_weight_grad = lax.psum_scatter(
        qkv_weight_grad.reshape(ctx_count, width // ctx_count, 3 * columns),
        plane,
        scatter_dimension=1,
        tiled=True,
    )
    qkv_weight_grad = lax.all_to_all(
        qkv_weight_grad, "ctx", split_axis=0, concat_axis=0, tiled=True
    )
    out_rows = qkv_weight_grad.shape[1]
    qkv_weight_grad = (
        qkv_weight_grad.reshape(ctx_count, out_rows, 3, columns)
        .transpose(2, 1, 0, 3)
        .reshape(3, out_rows, width)
        .astype(FLOAT)
    )
    input_part, attn_gain_grad = norm_backward(inputs, attn_inverse, attn_gain, attn_in_grad)
    input_grad = hidden_grad + input_part

    empty = jnp.zeros((width,), FLOAT)
    small = jnp.concatenate(
        [
            jnp.stack(
                [
                    attn_gain_grad,
                    lax.dynamic_update_slice_in_dim(empty, query_gain_grad, first_column, axis=0),
                    lax.dynamic_update_slice_in_dim(empty, key_gain_grad, first_column, axis=0),
                    mlp_gain_grad,
                ],
                axis=1,
            ),
            router_grad,
        ],
        axis=1,
    )
    small = lax.psum_scatter(small, everything, scatter_dimension=0, tiled=True)
    return (
        mixed.astype(BRAIN)[None],
        input_grad[None],
        qkv_weight_grad[0],
        qkv_weight_grad[1],
        qkv_weight_grad[2],
        out_weight_grad,
        small[:, 0],
        small[:, 1],
        small[:, 2],
        small[:, 3],
        small[:, 4:],
        gate_weight_grad,
        up_weight_grad,
        down_weight_grad,
    )


def solution(mesh):
    return jax.shard_map(
        shards,
        mesh=mesh,
        in_specs=(
            P(("dp", "expert"), "ctx", None),
            P(("dp", "expert"), "ctx", None),
            P(),
            P(),
            P(),
            P(),
            P(),
            P(),
            P(),
            P(),
            P(),
            P("expert", None, None),
            P("expert", None, None),
            P("expert", None, None),
            P(("dp", "expert"), "ctx", None),
        ),
        out_specs=(
            P(("dp", "expert"), "ctx", None),
            P(("dp", "expert"), "ctx", None),
            P(("ctx", "dp", "expert"), None),
            P(("ctx", "dp", "expert"), None),
            P(("ctx", "dp", "expert"), None),
            P(("ctx", "dp", "expert"), None),
            P(("ctx", "dp", "expert")),
            P(("ctx", "dp", "expert")),
            P(("ctx", "dp", "expert")),
            P(("ctx", "dp", "expert")),
            P(("ctx", "dp", "expert"), None),
            P("expert", ("ctx", "dp"), None),
            P("expert", ("ctx", "dp"), None),
            P("expert", ("ctx", "dp"), None),
        ),
        check_vma=False,
    )
```

time: 2980 us -> 1380 us (0.46)
  waiting for transfers between devices: 2310 us -> 805 us
  local copies, waits for them, and re-layouts: 181 us -> 74.2 us
  blocking collectives: 0 us -> 71.9 us
  other arithmetic: 106 us -> 60 us
    reduce_scatter x9 -> x8, waiting for transfers between devices: 1690 us -> 584 us  [the longest x3 309 us: spread(): lax.psum_scatter(partial.astype(BRAIN), 'ctx', scatter_dimension=1, tiled...]
    all_to_all x4, waiting for transfers between devices: 355 us -> 19.1 us  [the longest x3 19.1 us: spread(): lax.all_to_all(summed, 'dp', split_axis=1, concat_axis=0, tiled=True)]
    gather x2 -> x0, local copies, waits for them, and re-layouts: 44.5 us -> none  [the longest x1 22.3 us: shards(): returned_grads.reshape(experts_all * capacity, width)[flat_index]]
    all_gather x2 -> x4, waiting for transfers between devices: 110 us -> 67.6 us  [the longest x1 41.9 us: shards(): all_in = lax.all_gather(attn_in, 'ctx', axis=0, tiled=True)]
    all_to_all x0 -> x2, blocking collectives: none -> 35.9 us  [the longest x1 28.4 us: shards(): lax.all_to_all(attn_own, 'ctx', split_axis=0, concat_axis=1, tiled=True)]
    dot_general x28 -> x19, matrix products: 260 us -> 288 us  [the longest x1 39.3 us: shards(): jnp.einsum('td,edf->etf', all_expert_in, up_weights, preferred_element_ty...]
    unnamed x15 -> x14, waiting for transfers between devices: 160 us -> 134 us
  transfers between devices with their start and end apart: 17 -> 17, of which waited for: 17 -> 13; matrix products, arithmetic and copies ran while one was open for 12% -> 23% of each run, Pallas kernels for 0% -> 0%
where the time goes in v1:
time: 1380 us
  waiting for transfers between devices  805 us (58%)
  matrix products  332 us (24%)
  local copies, waits for them, and re-layouts  74.2 us (5%)
  blocking collectives  71.9 us (5%)
  other arithmetic  60 us (4%)
  starting transfers between devices  20.3 us (1%)
  between operations  15.1 us (1%)
    reduce_scatter x3, waiting for transfers between devices, spread(): lax.psum_scatter(partial.astype(BRAIN), 'ctx', scatter_dimension=1, tiled...  309 us
    unnamed x14, waiting for transfers between devices  134 us
    reduce_scatter x1, waiting for transfers between devices, shards(): lax.psum_scatter(times_transpose(qkv_low, qkv_weights).astype(BRAIN), 'ct...  77.2 us
    reduce_scatter x1, waiting for transfers between devices, shards(): lax.psum_scatter(produced, plane, scatter_dimension=0, tiled=True)  70 us
    reduce_scatter x1, waiting for transfers between devices, shards(): lax.psum_scatter(input_rows, plane, scatter_dimension=0, tiled=True)  63.9 us
    reduce_scatter x1, waiting for transfers between devices, shards(): lax.psum_scatter(qkv_weight_grad.reshape(ctx_count, width // ctx_count, 3...  62.1 us
    all_gather x1, waiting for transfers between devices, shards(): all_in = lax.all_gather(attn_in, 'ctx', axis=0, tiled=True)  41.9 us
    dot_general x1, matrix products, shards(): jnp.einsum('td,edf->etf', all_expert_in, up_weights, preferred_element_ty...  39.3 us
  transfers between devices with their start and end apart: 17, of which 13 were waited for; matrix products, arithmetic and copies ran while one was open for 23% of the time, Pallas kernels for 0%

profile of v1, /device:TPU:0, one launch (start us, length us, event | category | flops | bytes accessed | tf_op | source)
XLA Modules:
  0.0 1378.3 jit_solution(12923847066369536948)
XLA Ops:
  26.9 15.5 %all_gather.19 = f32[1024,2]{0,1:T(2,128)S(1)} all-gather(f32[256,2]{0,1:T(2,128)S(1)} %pad_maximum_fusion.8), channel_id=1, replica_groups=mesh['ctx'=4,'dp'=2,'expert'=4] {'ctx'}, dimensions={0}, use_global_device_ids=true | all-gather | bytes 10240 | tf_op jit(solution)/shard_map/all_gather | solution.py:119
  53.8 41.9 %all-gather.6.cloned.1.call-done = bf16[1024,2048]{1,0:T(8,128)(2,1)} async-done(((bf16[256,2048]{1,0:T(8,128)(2,1)}), bf16[1024,2048]{1,0:T(8,128)(2,1)}) %all-gather.6.cloned.1.call-update) | async-done | bytes 4194320 | tf_op jit(solution)/shard_map/all_gather | solution.py:101
  118.1 11.8 fusion.101
  144.4 28.4 %all_to_all.56 = bf16[4,256,512]{1,2,0:T(8,128)(2,1)S(1)} all-to-all(bf16[4,256,512]{1,2,0:T(8,128)(2,1)S(1)} %copy.175), channel_id=1, replica_groups=mesh['ctx'=4,'dp'=2,'expert'=4] {'ctx'}, dimensions={0} | all-to-all | bytes 2097152 | tf_op jit(solution)/shard_map/all_to_all | solution.py:155
  193.6 24.3 %fusion.13 = f32[2,1024,2048]{2,1,0:T(8,128)} fusion(bf16[1,2048,2048]{2,1,0:T(8,128)(2,1)} %all-gather.12.cloned.1.call-done, bf16[4,1024,2048]{2,1,0:T(8,128)(2,1)} %param.28, s32[]{:T(128)S(6)} %select_n.33), kind=kOutput, calls=%fused_computation.27 | convolution fusion | flops 17179869184 | bytes 33554436 | tf_op jit(solution)/shard_map/td,efd->etf/dot_general | solution.py:128
  218.0 16.7 %all-gather.8.cloned.1.call-done = bf16[2048,2048]{1,0:T(8,128)(2,1)} async-done(((bf16[256,2048]{1,0:T(8,128)(2,1)}), bf16[2048,2048]{1,0:T(8,128)(2,1)}) %all-gather.8.cloned.1.call-update) | async-done | bytes 8388624 | tf_op jit(solution)/shard_map/all_gather | solution.py:159
  234.7 24.4 %fusion.21 = f32[2,1024,2048]{2,1,0:T(8,128)} fusion(bf16[2048,2048]{1,0:T(8,128)(2,1)} %all-gather.8.cloned.1.call-done, bf16[4,2048,1024]{2,1,0:T(8,128)(2,1)} %param.26, s32[]{:T(128)S(6)} %select_n.33), kind=kOutput, calls=%fused_computation.35 | convolution fusion | flops 17179869184 | bytes 33554436 | tf_op jit(solution)/shard_map/td,edf->etf/dot_general | solution.py:170
  259.1 39.3 %fusion.5 = (bf16[2,2048,1024]{1,2,0:T(8,128)(2,1)}, f32[2,2048]{1,0:T(2,128)S(1)}, bf16[2,2048,1024]{1,2,0:T(8,128)(2,1)}, bf16[2,2048,1024]{1,2,0:T(8,128)(2,1)}) fusion(f32[2,1024,2048]{2,1,0:T(8,128)} %fusion.21, f32[2,1024,2048]{2,1,0:T(8,128)} %fusion.13, f32[2,2048]{1,0:T(2,128)S(1)} %dynamic-slice_bitcast_fusion, ...), kind=kOutput, calls=%fused_computation.11 | convolution fusion | flops 17259556864 | bytes 75530240 | tf_op jit(solution)/shard_map/td,edf->etf/dot_general | solution.py:173
  298.4 24.4 %fusion.31 = f32[2048,2048,1]{1,0,2:T(8,128)} fusion(bf16[2,2048,1024]{1,2,0:T(8,128)(2,1)} %get-tuple-element.24, bf16[4,2048,1024]{2,1,0:T(8,128)(2,1)} %param.26, s32[]{:T(128)S(6)} %select_n.33), kind=kOutput, calls=%fused_computation.49 | convolution fusion | flops 17179869184 | bytes 33554436 | tf_op jit(solution)/shard_map/etf,edf->td/dot_general | solution.py:185
  322.8 27.3 %fusion.1 = bf16[2048,2048]{1,0:T(8,128)(2,1)} fusion(f32[2048,2048,1]{1,0,2:T(8,128)} %fusion.31, bf16[2,2048,1024]{1,2,0:T(8,128)(2,1)} %get-tuple-element.26, bf16[4,2048,1024]{2,1,0:T(8,128)(2,1)} %param.27, s32[]{:T(128)S(6)} %select_n.33), kind=kOutput, calls=%fused_computation.2 | convolution fusion | flops 17188257792 | bytes 41943044 | tf_op jit(solution)/shard_map/etf,edf->td/dot_general | solution.py:186
  357.9 63.9 %reduce-scatter.14.cloned.1.call-done = bf16[256,2048]{1,0:T(8,128)(2,1)} async-done(((bf16[2048,2048]{1,0:T(8,128)(2,1)}), bf16[256,2048]{1,0:T(8,128)(2,1)}) %reduce-scatter.14.cloned.1.call-update) | async-done | bytes 1048592 | tf_op jit(solution)/shard_map/reduce_scatter | solution.py:188
  427.8 24.1 %convert_bitcast_fusion.1 = bf16[2,2048,1024]{1,2,0:T(8,128)(2,1)} fusion(bf16[2,2048,1024]{1,2,0:T(8,128)(2,1)} %get-tuple-element.24, bf16[2048,2048]{1,0:T(8,128)(2,1)} %all-gather.8.cloned.1.call-done), kind=kOutput, calls=%fused_computation.38 | convolution fusion | flops 17184063488 | bytes 25165824 | tf_op jit(solution)/shard_map/td,etf->edf/dot_general | solution.py:218
  451.9 23.7 %convert_bitcast_fusion = bf16[2,2048,1024]{1,2,0:T(8,128)(2,1)} fusion(bf16[2,2048,1024]{1,2,0:T(8,128)(2,1)} %get-tuple-element.26, bf16[2048,2048]{1,0:T(8,128)(2,1)} %all-gather.8.cloned.1.call-done), kind=kOutput, calls=%fused_computation.37 | convolution fusion | flops 17184063488 | bytes 25165824 | tf_op jit(solution)/shard_map/td,etf->edf/dot_general | solution.py:221
  475.7 23.7 %fusion.38 = bf16[2,1024,2048]{2,1,0:T(8,128)(2,1)} fusion(bf16[2,2048,1024]{1,2,0:T(8,128)(2,1)} %get-tuple-element.27, bf16[1,2048,2048]{2,1,0:T(8,128)(2,1)} %all-gather.12.cloned.1.call-done), kind=kOutput, calls=%fused_computation.53 | convolution fusion | flops 17184063488 | bytes 25165824 | tf_op jit(solution)/shard_map/etf,td->efd/dot_general | solution.py:215
  583.2 11.4 convolution_convert_fusion
  595.1 23.9 %bitcast_convert_fusion = bf16[2048,2048]{1,0:T(8,128)(2,1)} fusion(bf16[2,2048,1024]{1,2,0:T(8,128)(2,1)} %get-tuple-element.27, bf16[4,1024,2048]{2,1,0:T(8,128)(2,1)} %param.28, s32[]{:T(128)S(6)} %select_n.33), kind=kOutput, calls=%fused_computation.6 | convolution fusion | flops 17184063488 | bytes 25165828 | tf_op jit(solution)/shard_map/etf,efd->td/dot_general | solution.py:191
  619.0 35.5 %reduce-scatter.22.cloned.1.call-done = bf16[2,512,1024]{1,2,0:T(8,128)(2,1)} async-done(((bf16[2,2048,1024]{1,2,0:T(8,128)(2,1)}), bf16[2,512,1024]{1,2,0:T(8,128)(2,1)}) %reduce-scatter.22.cloned.1.call-update) | async-done | bytes 2097168 | tf_op jit(solution)/shard_map/reduce_scatter | solution.py:211
  664.8 137.3 %reduce-scatter.24.cloned.1.call-done = bf16[2,512,1024]{1,2,0:T(8,128)(2,1)} async-done(((bf16[2,2048,1024]{1,2,0:T(8,128)(2,1)}), bf16[2,512,1024]{1,2,0:T(8,128)(2,1)}) %reduce-scatter.24.cloned.1.call-update) | async-done | bytes 2097168 | tf_op jit(solution)/shard_map/reduce_scatter | solution.py:211
  813.7 136.0 %reduce-scatter.26.cloned.1.call-done = bf16[2,256,2048]{2,1,0:T(8,128)(2,1)} async-done(((bf16[2,1024,2048]{2,1,0:T(8,128)(2,1)}), bf16[2,256,2048]{2,1,0:T(8,128)(2,1)}) %reduce-scatter.26.cloned.1.call-update) | async-done | bytes 2097168 | tf_op jit(solution)/shard_map/reduce_scatter | solution.py:211
  970.9 19.1 %all-to-all-done.5 = bf16[2,256,2048]{2,0,1:T(2,128)(2,1)} async-done(((bf16[2,256,2048]{2,0,1:T(2,128)(2,1)}), bf16[2,256,2048]{2,0,1:T(2,128)(2,1)}, u32[]{:S(2)}, u32[]{:S(2)}) %all-to-all-start.5) | async-done | bytes 2097184 | tf_op jit(solution)/shard_map/all_to_all | solution.py:212
  1002.2 77.2 %reduce-scatter.16.cloned.1.call-done = bf16[256,2048]{1,0:T(8,128)(2,1)} async-done(((bf16[1024,2048]{1,0:T(8,128)(2,1)}), bf16[256,2048]{1,0:T(8,128)(2,1)}) %reduce-scatter.16.cloned.1.call-update) | async-done | bytes 1048592 | tf_op jit(solution)/shard_map/reduce_scatter | solution.py:278
  1083.0 62.1 %reduce-scatter.18.cloned.1.call-done = bf16[4,64,1536]{2,1,0:T(8,128)(2,1)} async-done(((bf16[4,512,1536]{2,1,0:T(8,128)(2,1)}), bf16[4,64,1536]{2,1,0:T(8,128)(2,1)}) %reduce-scatter.18.cloned.1.call-update) | async-done | bytes 786448 | tf_op jit(solution)/shard_map/reduce_scatter | solution.py:282
  1150.0 70.0 %reduce-scatter.12.cloned.1.call-done = bf16[256,2048]{1,0:T(8,128)(2,1)} async-done(((bf16[2048,2048]{1,0:T(8,128)(2,1)}), bf16[256,2048]{1,0:T(8,128)(2,1)}) %reduce-scatter.12.cloned.1.call-update) | async-done | bytes 1048592 | tf_op jit(solution)/shard_map/reduce_scatter | solution.py:194
  1225.5 133.2 %reduce-scatter.28.cloned.1.call-done = f32[64,20]{1,0:T(8,128)} async-done(((f32[2048,20]{1,0:T(8,128)}), f32[64,20]{1,0:T(8,128)}) %reduce-scatter.28.cloned.1.call-update) | async-done | bytes 5136
  (282 shorter events, 268.1 us)
Async XLA Ops:
  7.2 174.1 %copy-start = (bf16[2048,16]{0,1:T(8,128)(2,1)S(1)}, bf16[2048,16]{0,1:T(8,128)(2,1)}, u32[]{:S(2)}) copy-start(bf16[2048,16]{0,1:T(8,128)(2,1)} %param.25) | copy-start | bytes 196612
  7.2 88.4 %all-gather.6.cloned.1.call-start = ((), (), s32[]{:S(2)}) async-start(), calls=%async_computation.15 | async-start | bytes 5242880 | tf_op jit(solution)/shard_map/all_gather | solution.py:101
  11.9 181.7 %all-gather.12.cloned.1.call-start = ((), (), s32[]{:S(2)}) async-start(), calls=%async_computation.26 | async-start | bytes 9437184 | tf_op jit(solution)/shard_map/all_gather | solution.py:104
  12.6 222.0 %all-gather.8.cloned.1.call-start = ((), (), s32[]{:S(2)}) async-start(), calls=%async_computation.16 | async-start | bytes 9437184 | tf_op jit(solution)/shard_map/all_gather | solution.py:159
  181.2 240.7 %reduce-scatter.14.cloned.1.call-start = ((), (), s32[]{:S(2)}) async-start(), calls=%async_computation.18 | async-start | bytes 9437184 | tf_op jit(solution)/shard_map/reduce_scatter | solution.py:188
  350.2 158.4 %all-gather.10.cloned.1.call-start = ((), (), s32[]{:S(2)}) async-start(), calls=%async_computation.19 | async-start | bytes 5242880 | tf_op jit(solution)/shard_map/all_gather | solution.py:233
  427.7 226.7 %reduce-scatter.22.cloned.1.call-start = ((), (), s32[]{:S(2)}) async-start(), calls=%async_computation.23 | async-start | bytes 10485760 | tf_op jit(solution)/shard_map/reduce_scatter | solution.py:211
  451.9 350.2 %reduce-scatter.24.cloned.1.call-start = ((), (), s32[]{:S(2)}) async-start(), calls=%async_computation.24 | async-start | bytes 10485760 | tf_op jit(solution)/shard_map/reduce_scatter | solution.py:211
  475.6 474.0 %reduce-scatter.26.cloned.1.call-start = ((), (), s32[]{:S(2)}) async-start(), calls=%async_computation.25 | async-start | bytes 10485760 | tf_op jit(solution)/shard_map/reduce_scatter | solution.py:211
  499.4 501.1 %reduce-scatter.20.cloned.1.call-start = ((), (), s32[]{:S(2)}) async-start(), calls=%async_computation.22 | async-start | bytes 2359296 | tf_op jit(solution)/shard_map/reduce_scatter | solution.py:236
  536.7 542.7 %reduce-scatter.16.cloned.1.call-start = ((), (), s32[]{:S(2)}) async-start(), calls=%async_computation.20 | async-start | bytes 5242880 | tf_op jit(solution)/shard_map/reduce_scatter | solution.py:278
  581.6 563.4 %reduce-scatter.18.cloned.1.call-start = ((), (), s32[]{:S(2)}) async-start(), calls=%async_computation.21 | async-start | bytes 7077888 | tf_op jit(solution)/shard_map/reduce_scatter | solution.py:282
  594.6 625.3 %reduce-scatter.12.cloned.1.call-start = ((), (), s32[]{:S(2)}) async-start(), calls=%async_computation.17 | async-start | bytes 9437184 | tf_op jit(solution)/shard_map/reduce_scatter | solution.py:194
  660.7 147.6 %all-to-all-start.3 = ((bf16[2,512,1024]{2,0,1:T(2,128)(2,1)}), bf16[2,512,1024]{2,0,1:T(2,128)(2,1)S(1)}, u32[]{:S(2)}, u32[]{:S(2)}) async-start(bf16[2,512,1024]{2,0,1:T(2,128)(2,1)} %copy.196), calls=%async_computation.9 | async-start | bytes 4194304 | tf_op jit(solution)/shard_map/all_to_all | solution.py:212
  664.7 148.7 %copy-start.11 = (bf16[256,2048]{1,0:T(8,128)(2,1)S(1)}, bf16[256,2048]{1,0:T(8,128)(2,1)}, u32[]{:S(2)}) copy-start(bf16[256,2048]{1,0:T(8,128)(2,1)} %multiply_convert_fusion.3) | copy-start | bytes 3145732
  664.7 148.7 %copy-start.38 = (bf16[256,16]{0,1:T(8,128)(2,1)S(1)}, bf16[256,16]{0,1:T(8,128)(2,1)}, u32[]{:S(2)}) copy-start(bf16[256,16]{0,1:T(8,128)(2,1)} %copy-done.37) | copy-start | bytes 24580
  808.3 146.5 %all-to-all-start.4 = ((bf16[2,512,1024]{2,0,1:T(2,128)(2,1)}), bf16[2,512,1024]{2,0,1:T(2,128)(2,1)}, u32[]{:S(2)}, u32[]{:S(2)}) async-start(bf16[2,512,1024]{2,0,1:T(2,128)(2,1)} %copy.198), calls=%async_computation.11 | async-start | bytes 4194304 | tf_op jit(solution)/shard_map/all_to_all | solution.py:212
  954.8 35.2 %all-to-all-start.5 = ((bf16[2,256,2048]{2,0,1:T(2,128)(2,1)}), bf16[2,256,2048]{2,0,1:T(2,128)(2,1)}, u32[]{:S(2)}, u32[]{:S(2)}) async-start(bf16[2,256,2048]{2,0,1:T(2,128)(2,1)} %copy.200), calls=%async_computation.13 | async-start | bytes 4194304 | tf_op jit(solution)/shard_map/all_to_all | solution.py:212
  959.6 399.2 %reduce-scatter.28.cloned.1.call-start = ((), (), s32[]{:S(2)}) async-start(), calls=%async_computation.27 | async-start | bytes 1081344
  998.5 221.4 %copy-start.5 = (f32[256,2048]{1,0:T(8,128)S(1)}, f32[256,2048]{1,0:T(8,128)}, u32[]{:S(2)}) copy-start(f32[256,2048]{1,0:T(8,128)} %copy-done.3) | copy-start | bytes 6291460
  998.5 221.4 %copy-start.36 = (f32[2048]{0:T(1024)S(1)}, f32[2048]{0:T(1024)}, u32[]{:S(2)}) copy-start(f32[2048]{0:T(1024)} %param.24) | copy-start | bytes 24580
  998.5 221.4 %copy-start.57 = (f32[256]{0:T(256)S(1)}, f32[256]{0:T(256)}, u32[]{:S(2)}) copy-start(f32[256]{0:T(256)} %copy-done.55) | copy-start | bytes 3076
  998.5 221.4 %copy-start.65 = (f32[256]{0:T(256)S(1)}, f32[256]{0:T(256)}, u32[]{:S(2)}) copy-start(f32[256]{0:T(256)} %copy-done.64) | copy-start | bytes 3076
  1145.1 218.5 %all-to-all-start.2 = ((bf16[4,64,1536]{2,1,0:T(8,128)(2,1)}), bf16[4,64,1536]{2,1,0:T(8,128)(2,1)}, u32[]{:S(2)}, u32[]{:S(2)}) async-start(bf16[4,64,1536]{2,1,0:T(8,128)(2,1)} %reduce-scatter.18.cloned.1.call-done), calls=%async_computation.6 | async-start | bytes 1572864 | tf_op jit(solution)/shard_map/all_to_all | solution.py:288
  (65 other events, 1368.2 us)
Sparse Core Ops, SparseCore 0:
  12.0 83.5 all-gather.5
  97.5 52.7 all-gather.11
  181.3 53.3 all-gather.7
  350.3 71.4 reduce-scatter.13
  427.8 80.7 all-gather.9
  510.8 143.5 reduce-scatter.21
  656.8 145.2 reduce-scatter.23
  804.4 145.2 reduce-scatter.25
  953.0 47.4 reduce-scatter.19
  1002.6 76.7 reduce-scatter.15
  1082.8 62.2 reduce-scatter.17
  1148.4 71.4 reduce-scatter.11
  1222.2 136.5 reduce-scatter.27
